TPU v7x, 32 devices: a whole 2x2x4 slice. The times are simulated.
32 devices in a mesh: groups: 2 (over y), streams: 8 (over z, x), segment: 2 (over core).
Axes of the slice: x: 2, y: 2, z: 4, core: 2. Of those that a mesh axis runs over, the one named last changes fastest.
Arguments:
- latent: bfloat16 [4096, 1024], P(('groups', 'streams'), 'segment'), parts along dimension 0, may hold values from -6 to 6
- conv_weight: bfloat16 [1024, 16, 512], P('streams', None, 'segment'), may hold values from -0.1875 to 0.1875
- conv_bias: float32 [512], P('segment'), may hold values from -3 to 3
- tail_cache: bfloat16 [128, 8, 512], P(('groups', 'streams'), None, 'segment'), parts along dimension 0, may hold values from -6 to 6
- input_cache: bfloat16 [128, 2, 512], P(('groups', 'streams'), None, 'segment'), parts along dimension 0, may hold values from -0.8984375 to 2
- resume_slot: int32 [128], P(('groups', 'streams')), parts along dimension 0, may hold values from -1 to 255, as said below
- res_weight: bfloat16 [3, 512, 256], P(None, 'segment'), may hold values from -0.15625 to 0.15625
- res_bias: float32 [256], replicated, may hold values from -3 to 3
- skip_weight: bfloat16 [256, 512], P(None, 'segment'), may hold values from -0.375 to 0.375
- skip_bias: float32 [512], P('segment'), may hold values from -3 to 3
Outputs:
- decoded: bfloat16 [4096, 8, 512], P(('groups', 'streams'), None, 'segment'), parts along dimension 0
- new_tail: bfloat16 [4096, 8, 512], P(('groups', 'streams'), None, 'segment'), parts along dimension 0
There are 2 independent parts, one for each index of `groups`. A program takes and returns all parts, laid end to end along the dimension named above; an argument that names none is the same for every part. Nothing has to cross between parts.
Inputs may be any that keep to these rules, and one draw needn't show every extreme that they name: `resume_slot`: slot k of an owner device's store serves decoder device k // 1 of the same index range; an entry is -1 (slot unused) or the position, among that decoder device's 256 rows in decoder order, of the session that resumes from it. No decoder row is named by two slots. In every draw there is one decoder device all of whose reserved slots are in use (none is -1).
All inputs are finite; a program needn't handle non-finite values.
Results may differ from a plain program's by a relative error of at most 0.0042.
Values may be sent and summed in bfloat16 or wider, within the bound.
A program may use at most 64 MiB of HBM per device.

v0:
```python
import jax
import jax.numpy as jnp
from jax import lax
from jax.sharding import PartitionSpec as P


def apply_elu(values):
    return jnp.where(values > 0, values, jnp.expm1(jnp.minimum(values, 0.0)))


def local(
    latent,
    conv_weight,
    conv_bias,
    tail_cache,
    input_cache,
    resume_slot,
    res_weight,
    res_bias,
    skip_weight,
    skip_bias,
):
    handed = lax.all_to_all(latent, "streams", split_axis=0, concat_axis=0, tiled=True)
    excitation_half = apply_elu(handed.astype(jnp.float32)).astype(jnp.bfloat16)
    excitation = lax.all_gather(excitation_half, "segment", axis=1, tiled=True)
    session_rows = excitation.shape[0]
    tap_count = conv_weight.shape[1]
    half_taps = tap_count // 2
    half_width = conv_weight.shape[2]
    piece = lax.all_gather(conv_weight, "streams", axis=0, tiled=True)
    kernel_rows = piece.reshape(piece.shape[0], tap_count * half_width)
    spread = jnp.dot(excitation, kernel_rows, preferred_element_type=jnp.float32)
    spread = spread.reshape(session_rows, tap_count, half_width)
    fetched_tail, fetched_input, fetched_slot = (
        lax.all_to_all(tail_cache, "streams", split_axis=0, concat_axis=0, tiled=True),
        lax.all_to_all(input_cache, "streams", split_axis=0, concat_axis=0, tiled=True),
        lax.all_to_all(resume_slot, "streams", split_axis=0, concat_axis=0, tiled=True),
    )
    arrivals = fetched_slot.shape[0]
    state_steps = fetched_input.shape[1]
    packed = jnp.concatenate(
        [fetched_tail.reshape(arrivals, -1), fetched_input.reshape(arrivals, -1)], axis=1
    )
    one_hot = (fetched_slot[None, :] == jnp.arange(session_rows, dtype=jnp.int32)[:, None]).astype(
        jnp.bfloat16
    )
    placed = jnp.dot(one_hot, packed, preferred_element_type=jnp.float32)
    prev_tail = placed[:, : half_taps * half_width].reshape(session_rows, half_taps, half_width)
    prev_input = (
        placed[:, half_taps * half_width :]
        .reshape(session_rows, state_steps, half_width)
        .astype(jnp.bfloat16)
    )
    upsampled = spread[:, :half_taps] + prev_tail + conv_bias
    new_tail = spread[:, half_taps:].astype(jnp.bfloat16)
    excited = apply_elu(upsampled).astype(jnp.bfloat16)
    window = jnp.concatenate([prev_input, excited], axis=1)
    hidden_width = res_weight.shape[2]
    partial_value = jnp.zeros((session_rows * half_taps, hidden_width), jnp.float32)
    for offset in range(res_weight.shape[0]):
        frames = window[:, offset : offset + half_taps].reshape(
            session_rows * half_taps, half_width
        )
        partial_value = partial_value + jnp.dot(
            frames, res_weight[offset], preferred_element_type=jnp.float32
        )
    partial_value = partial_value.reshape(session_rows, half_taps, hidden_width)
    summed = lax.psum(partial_value, "segment")
    hidden = apply_elu(summed + res_bias).astype(jnp.bfloat16)
    projected = jnp.dot(
        hidden.reshape(session_rows * half_taps, hidden_width),
        skip_weight,
        preferred_element_type=jnp.float32,
    )
    decoded_block = upsampled + projected.reshape(session_rows, half_taps, half_width) + skip_bias
    return (decoded_block.astype(jnp.bfloat16), new_tail)


def solution(mesh):
    placed = (
        P(("groups", "streams"), "segment"),
        P("streams", None, "segment"),
        P("segment"),
        P(("groups", "streams"), None, "segment"),
        P(("groups", "streams"), None, "segment"),
        P(("groups", "streams")),
        P(None, "segment", None),
        P(),
        P(None, "segment"),
        P("segment"),
    )
    return jax.shard_map(
        local,
        mesh=mesh,
        in_specs=placed,
        out_specs=(
            P(("groups", "streams"), None, "segment"),
            P(("groups", "streams"), None, "segment"),
        ),
        check_vma=False,
    )
```

profile of v0, /device:TPU:0, one launch (start us, length us, event | category | flops | bytes accessed | tf_op | source)
XLA Modules:
  0.0 200.5 jit_solution(6672146681331437145)
XLA Ops:
  7.2 0.7 all-gather.2.cloned.1.call-update
  7.9 0.7 copy.39
  8.6 13.6 %all_to_all.28 = s32[8,1,1]{2,1,0:T(1,128)S(1)} all-to-all(s32[8,1,1]{2,1,0:T(1,128)S(1)} %copy.39), channel_id=1, replica_groups=mesh['groups'=2,'streams'=8,'segment'=2] {'streams'}, dimensions={0} | all-to-all | bytes 64 | tf_op jit(solution)/shard_map/all_to_all | solution.py:37
  22.2 10.1 %all_to_all.29 = bf16[8,2,256]{2,1,0:T(2,128)(2,1)S(1)} all-to-all(bf16[8,2,256]{2,1,0:T(2,128)(2,1)} %param.14), channel_id=1, replica_groups=mesh['groups'=2,'streams'=8,'segment'=2] {'streams'}, dimensions={0} | all-to-all | bytes 16384 | tf_op jit(solution)/shard_map/all_to_all | solution.py:36
  32.3 10.5 %all_to_all.30 = bf16[8,8,256]{2,1,0:T(8,128)(2,1)S(1)} all-to-all(bf16[8,8,256]{2,1,0:T(8,128)(2,1)} %param.13), channel_id=1, replica_groups=mesh['groups'=2,'streams'=8,'segment'=2] {'streams'}, dimensions={0} | all-to-all | bytes 65536 | tf_op jit(solution)/shard_map/all_to_all | solution.py:35
  42.8 3.4 %all-to-all-start = ((bf16[8,32,512]{2,1,0:T(8,128)(2,1)}), bf16[8,32,512]{2,1,0:T(8,128)(2,1)S(1)}, u32[]{:S(2)}, u32[]{:S(2)}) async-start(bf16[8,32,512]{2,1,0:T(8,128)(2,1)} %bitcast.46), calls=%async_computation | async-start | bytes 524288 | tf_op jit(solution)/shard_map/all_to_all | solution.py:23
  46.3 0.2 reduce
  46.5 0.5 fusion.27
  47.1 0.2 slice.39
  47.2 1.9 copy.40
  49.1 1.9 copy.41
  51.0 0.1 copy.42
  51.2 0.1 copy.43
  51.3 10.6 %all-to-all-done = bf16[8,32,512]{2,1,0:T(8,128)(2,1)S(1)} async-done(((bf16[8,32,512]{2,1,0:T(8,128)(2,1)}), bf16[8,32,512]{2,1,0:T(8,128)(2,1)S(1)}, u32[]{:S(2)}, u32[]{:S(2)}) %all-to-all-start) | async-done | bytes 262176 | tf_op jit(solution)/shard_map/all_to_all | solution.py:23
  61.9 0.2 fusion.18
  62.1 2.4 %all_gather.6 = bf16[256,1024]{1,0:T(8,128)(2,1)S(1)} all-gather(bf16[256,512]{1,0:T(8,128)(2,1)S(1)} %fusion.18), channel_id=1, replica_groups=mesh['groups'=2,'streams'=8,'segment'=2] {'segment'}, dimensions={1}, use_global_device_ids=true | all-gather | bytes 786432 | tf_op jit(solution)/shard_map/all_gather | solution.py:25
  64.5 79.3 %all-gather.2.cloned.1.call-done = bf16[1024,16,256]{2,1,0:T(8,128)(2,1)} async-done(((bf16[128,16,256]{2,1,0:T(8,128)(2,1)}), bf16[1024,16,256]{2,1,0:T(8,128)(2,1)}) %all-gather.2.cloned.1.call-update) | async-done | bytes 8388624 | tf_op jit(solution)/shard_map/all_gather | solution.py:30
  143.7 12.3 %copy.50 = bf16[1024,16,256]{0,2,1:T(8,128)(2,1)} copy(bf16[1024,16,256]{2,1,0:T(8,128)(2,1)} %all-gather.2.cloned.1.call-done) | data formatting | bytes 16777216 | tf_op jit(solution)/shard_map/reshape | solution.py:31
  156.0 5.8 %fusion = f32[256,16,256]{2,0,1:T(8,128)S(1)} fusion(bf16[1024,16,256]{0,2,1:T(8,128)(2,1)} %copy.50, bf16[256,1024]{1,0:T(8,128)(2,1)S(1)} %all_gather.6), kind=kOutput, calls=%fused_computation | convolution fusion | flops 2147483648 | bytes 13107200 | tf_op jit(solution)/shard_map/dot_general | solution.py:32
  161.8 1.0 fusion.2
  162.7 1.0 copy-done.1
  163.7 0.1 pad_maximum_fusion
  163.9 0.9 copy-done.2
  164.7 0.7 fusion.10
  165.4 0.8 convolution_add_fusion.1
  166.2 0.8 fusion.5
  167.0 2.0 copy.47
  169.0 1.7 slice.71
  170.8 1.6 copy.49
  172.3 16.3 %all-reduce.2.cloned.1.call-done = f32[256,8,256]{2,0,1:T(8,128)} async-done(((f32[256,8,256]{2,0,1:T(8,128)}), f32[256,8,256]{2,0,1:T(8,128)}) %all-reduce.2.cloned.1.call-update) | async-done | bytes 2097168 | tf_op jit(solution)/shard_map/psum | solution.py:68
  188.7 3.4 %add_convert_fusion = bf16[256,8,256]{2,0,1:T(8,128)(2,1)S(1)} fusion(f32[256,8,256]{2,0,1:T(8,128)} %all-reduce.2.cloned.1.call-done, f32[256]{0:T(256)S(1)} %copy-done.4, f32[256]{0:T(256)S(1)} %copy-done.5, f32[256]{0:T(256)S(1)} %copy-done.3, f32[256,8,256]{2,0,1:T(8,128)S(1)} %copy.41, f32[256,16,256]{2,0,1:T(8,128)} %copy-done.1, ...), kind=kOutput, calls=%fused_computation.11 | convolution fusion | flops 273678336 | bytes 7474176 | tf_op jit(solution)/shard_map/dot_general | solution.py:70
  192.1 1.6 copy.48
  (16 shorter events, 0.2 us)
Async XLA Ops:
  7.2 181.5 %copy-start = (bf16[256,256]{1,0:T(8,128)(2,1)S(1)}, bf16[256,256]{1,0:T(8,128)(2,1)}, u32[]{:S(2)}) copy-start(bf16[256,256]{1,0:T(8,128)(2,1)} %param.18) | copy-start | bytes 393220
  7.2 136.5 %all-gather.2.cloned.1.call-start = ((), (), s32[]{:S(2)}) async-start(), calls=%async_computation.4 | async-start | bytes 9437184 | tf_op jit(solution)/shard_map/all_gather | solution.py:30
  42.8 19.1 %all-to-all-start = ((bf16[8,32,512]{2,1,0:T(8,128)(2,1)}), bf16[8,32,512]{2,1,0:T(8,128)(2,1)S(1)}, u32[]{:S(2)}, u32[]{:S(2)}) async-start(bf16[8,32,512]{2,1,0:T(8,128)(2,1)} %bitcast.46), calls=%async_computation | async-start | bytes 524288 | tf_op jit(solution)/shard_map/all_to_all | solution.py:23
  46.2 142.4 %all-reduce.2.cloned.1.call-start = ((), (), s32[]{:S(2)}) async-start(), calls=%async_computation.5 | async-start | bytes 4194304 | tf_op jit(solution)/shard_map/psum | solution.py:68
  156.0 5.8 %copy-start.3 = (f32[256]{0:T(256)S(1)}, f32[256]{0:T(256)}, u32[]{:S(2)}) copy-start(f32[256]{0:T(256)} %param.12) | copy-start | bytes 3076
  161.8 1.9 copy-start.1
  163.7 1.0 copy-start.2
  169.0 19.6 %copy-start.4 = (f32[256]{0:T(256)S(1)}, f32[256]{0:T(256)}, u32[]{:S(2)}) copy-start(f32[256]{0:T(256)} %param.19) | copy-start | bytes 3076
  169.0 19.6 %copy-start.5 = (f32[256]{0:T(256)S(1)}, f32[256]{0:T(256)}, u32[]{:S(2)}) copy-start(f32[256]{0:T(256)} %param.17) | copy-start | bytes 3076
Sparse Core Ops, SparseCore 0:
  10.1 133.5 all-gather.1
  169.1 19.4 all-reduce.1
where the time goes:
time: 201 us; the launch traced here: 200 us
  waiting for transfers between devices  107 us (53%)
  blocking collectives  36.5 us (18%)
  local copies, waits for them, and re-layouts  25.9 us (13%)
  between operations  14.2 us (7%)
  matrix products  11.9 us (6%)
  starting transfers between devices  3.49 us (2%)
    all_gather x1, waiting for transfers between devices, local(): piece = lax.all_gather(conv_weight, 'streams', axis=0, tiled=True)  79.3 us
    psum x1, waiting for transfers between devices, local(): summed = lax.psum(partial_value, 'segment')  16.3 us
    all_to_all x1, blocking collectives, local(): lax.all_to_all(resume_slot, 'streams', split_axis=0, concat_axis=0, tiled...  13.6 us
    reshape x1, local copies, waits for them, and re-layouts, local(): kernel_rows = piece.reshape(piece.shape[0], tap_count * half_width)  12.3 us
    all_to_all x1, waiting for transfers between devices, local(): lax.all_to_all(latent, 'streams', split_axis=0, concat_axis=0, tiled=True)  10.6 us
    all_to_all x1, blocking collectives, local(): lax.all_to_all(tail_cache, 'streams', split_axis=0, concat_axis=0, tiled=...  10.5 us
    all_to_all x1, blocking collectives, local(): lax.all_to_all(input_cache, 'streams', split_axis=0, concat_axis=0, tiled...  10.1 us
    dot_general x1, matrix products, local(): jnp.dot(excitation, kernel_rows, preferred_element_type=jnp.float32)  5.76 us
  transfers between devices with their start and end apart: 3, of which 3 were waited for; matrix products, arithmetic and copies ran while one was open for 5% of the time, Pallas kernels for 0%

commit v1 on v0

--- a/solution.py
+++ b/solution.py
@@ -65,7 +65,7 @@
             frames, res_weight[offset], preferred_element_type=jnp.float32
         )
     partial_value = partial_value.reshape(session_rows, half_taps, hidden_width)
-    summed = lax.psum(partial_value, "segment")
+    summed = jnp.sum(lax.all_gather(partial_value, "segment"), axis=0)
     hidden = apply_elu(summed + res_bias).astype(jnp.bfloat16)
     projected = jnp.dot(
         hidden.reshape(session_rows * half_taps, hidden_width),

time: 201 us -> 197 us (0.980)
  waiting for transfers between devices: 107 us -> 99.2 us
  other arithmetic: 1.57 us -> 5.65 us
    psum x1 -> x0, waiting for transfers between devices: 16.3 us -> none  [local(): summed = lax.psum(partial_value, 'segment')]
    all_gather x0 -> x1, waiting for transfers between devices: none -> 8.72 us  [local(): summed = jnp.sum(lax.all_gather(partial_value, 'segment'), axis=0)]
    reduce_sum x0 -> x1, other arithmetic: none -> 4.08 us  [local(): summed = jnp.sum(lax.all_gather(partial_value, 'segment'), axis=0)]
where the time goes in v1:
time: 197 us
  waiting for transfers between devices  99.2 us (50%)
  blocking collectives  36.5 us (19%)
  local copies, waits for them, and re-layouts  23.9 us (12%)
  between operations  14.2 us (7%)
  matrix products  13.5 us (7%)
  other arithmetic  5.65 us (3%)
  starting transfers between devices  3.49 us (2%)
    all_gather x1, waiting for transfers between devices, local(): piece = lax.all_gather(conv_weight, 'streams', axis=0, tiled=True)  79.3 us
    all_to_all x1, blocking collectives, local(): lax.all_to_all(resume_slot, 'streams', split_axis=0, concat_axis=0, tiled...  13.6 us
    reshape x1, local copies, waits for them, and re-layouts, local(): kernel_rows = piece.reshape(piece.shape[0], tap_count * half_width)  12.3 us
    all_to_all x1, waiting for transfers between devices, local(): lax.all_to_all(latent, 'streams', split_axis=0, concat_axis=0, tiled=True)  10.6 us
    all_to_all x1, blocking collectives, local(): lax.all_to_all(tail_cache, 'streams', split_axis=0, concat_axis=0, tiled=...  10.5 us
    all_to_all x1, blocking collectives, local(): lax.all_to_all(input_cache, 'streams', split_axis=0, concat_axis=0, tiled...  10.1 us
    all_gather x1, waiting for transfers between devices, local(): summed = jnp.sum(lax.all_gather(partial_value, 'segment'), axis=0)  8.72 us
    dot_general x1, matrix products, local(): jnp.dot(excitation, kernel_rows, preferred_element_type=jnp.float32)  5.76 us
  transfers between devices with their start and end apart: 3, of which 3 were waited for; matrix products, arithmetic and copies ran while one was open for 5% of the time, Pallas kernels for 0%

profile of v1, /device:TPU:0, one launch (start us, length us, event | category | flops | bytes accessed | tf_op | source)
XLA Modules:
  0.0 196.5 jit_solution(5465649629616151837)
XLA Ops:
  7.2 0.7 all-gather.3.cloned.1.call-update
  7.9 0.7 copy.38
  8.6 13.6 %all_to_all.28 = s32[8,1,1]{2,1,0:T(1,128)S(1)} all-to-all(s32[8,1,1]{2,1,0:T(1,128)S(1)} %copy.38), channel_id=1, replica_groups=mesh['groups'=2,'streams'=8,'segment'=2] {'streams'}, dimensions={0} | all-to-all | bytes 64 | tf_op jit(solution)/shard_map/all_to_all | solution.py:37
  22.2 10.1 %all_to_all.29 = bf16[8,2,256]{2,1,0:T(2,128)(2,1)S(1)} all-to-all(bf16[8,2,256]{2,1,0:T(2,128)(2,1)} %param.14), channel_id=1, replica_groups=mesh['groups'=2,'streams'=8,'segment'=2] {'streams'}, dimensions={0} | all-to-all | bytes 16384 | tf_op jit(solution)/shard_map/all_to_all | solution.py:36
  32.3 10.5 %all_to_all.30 = bf16[8,8,256]{2,1,0:T(8,128)(2,1)S(1)} all-to-all(bf16[8,8,256]{2,1,0:T(8,128)(2,1)} %param.13), channel_id=1, replica_groups=mesh['groups'=2,'streams'=8,'segment'=2] {'streams'}, dimensions={0} | all-to-all | bytes 65536 | tf_op jit(solution)/shard_map/all_to_all | solution.py:35
  42.8 3.4 %all-to-all-start = ((bf16[8,32,512]{2,1,0:T(8,128)(2,1)}), bf16[8,32,512]{2,1,0:T(8,128)(2,1)S(1)}, u32[]{:S(2)}, u32[]{:S(2)}) async-start(bf16[8,32,512]{2,1,0:T(8,128)(2,1)} %bitcast.46), calls=%async_computation | async-start | bytes 524288 | tf_op jit(solution)/shard_map/all_to_all | solution.py:23
  46.3 0.2 reduce
  46.5 0.5 fusion.27
  47.1 0.2 slice.39
  47.2 1.9 copy.39
  49.1 1.9 copy.40
  51.0 0.1 copy.41
  51.2 0.1 copy.42
  51.3 10.6 %all-to-all-done = bf16[8,32,512]{2,1,0:T(8,128)(2,1)S(1)} async-done(((bf16[8,32,512]{2,1,0:T(8,128)(2,1)}), bf16[8,32,512]{2,1,0:T(8,128)(2,1)S(1)}, u32[]{:S(2)}, u32[]{:S(2)}) %all-to-all-start) | async-done | bytes 262176 | tf_op jit(solution)/shard_map/all_to_all | solution.py:23
  61.9 0.2 fusion.18
  62.1 2.4 %all_gather.9 = bf16[256,1024]{1,0:T(8,128)(2,1)S(1)} all-gather(bf16[256,512]{1,0:T(8,128)(2,1)S(1)} %fusion.18), channel_id=1, replica_groups=mesh['groups'=2,'streams'=8,'segment'=2] {'segment'}, dimensions={1}, use_global_device_ids=true | all-gather | bytes 786432 | tf_op jit(solution)/shard_map/all_gather | solution.py:25
  64.5 79.3 %all-gather.3.cloned.1.call-done = bf16[1024,16,256]{2,1,0:T(8,128)(2,1)} async-done(((bf16[128,16,256]{2,1,0:T(8,128)(2,1)}), bf16[1024,16,256]{2,1,0:T(8,128)(2,1)}) %all-gather.3.cloned.1.call-update) | async-done | bytes 8388624 | tf_op jit(solution)/shard_map/all_gather | solution.py:30
  143.7 12.3 %copy.49 = bf16[1024,16,256]{0,2,1:T(8,128)(2,1)} copy(bf16[1024,16,256]{2,1,0:T(8,128)(2,1)} %all-gather.3.cloned.1.call-done) | data formatting | bytes 16777216 | tf_op jit(solution)/shard_map/reshape | solution.py:31
  156.0 5.8 %fusion = f32[256,16,256]{2,0,1:T(8,128)S(1)} fusion(bf16[1024,16,256]{0,2,1:T(8,128)(2,1)} %copy.49, bf16[256,1024]{1,0:T(8,128)(2,1)S(1)} %all_gather.9), kind=kOutput, calls=%fused_computation | convolution fusion | flops 2147483648 | bytes 13107200 | tf_op jit(solution)/shard_map/dot_general | solution.py:32
  161.8 1.0 fusion.2
  162.7 1.0 copy-done.1
  163.7 0.1 pad_maximum_fusion
  163.9 0.9 copy-done.2
  164.7 0.7 fusion.10
  165.4 0.8 convolution_add_fusion.1
  166.2 2.2 %fusion.5 = f32[1,256,8,256]{3,2,1,0:T(8,128)} fusion(f32[2048,256]{1,0:T(8,128)S(1)} %convolution_add_fusion.1, bf16[256,8,256]{2,0,1:T(8,128)(2,1)S(1)} %fusion.2, bf16[3,256,256]{2,1,0:T(8,128)(2,1)S(1)} %copy-done.2), kind=kOutput, calls=%fused_computation.13 | convolution fusion | flops 268959744 | bytes 5373952 | tf_op jit(solution)/shard_map/dot_general | solution.py:64
  168.4 1.7 slice.71
  170.1 1.6 copy.48
  171.7 8.7 %all-gather.5.cloned.1.call-done = f32[2,256,8,256]{3,2,1,0:T(8,128)} async-done(((f32[1,256,8,256]{3,2,1,0:T(8,128)}), f32[2,256,8,256]{3,2,1,0:T(8,128)}) %all-gather.5.cloned.1.call-update) | async-done | bytes 4194320 | tf_op jit(solution)/shard_map/all_gather | solution.py:68
  180.4 4.1 %reduce_sum.9 = f32[256,8,256]{2,1,0:T(8,128)} reduce(f32[2,256,8,256]{3,2,1,0:T(8,128)} %all-gather.5.cloned.1.call-done, f32[]{:T(128)} %constant.1.clone.1), dimensions={0}, to_apply=%region_0.1 | reduce | flops 524288 | bytes 6291460 | tf_op jit(solution)/shard_map/reduce_sum | solution.py:68
  184.5 3.6 %add_convert_fusion = bf16[256,8,256]{2,0,1:T(8,128)(2,1)S(1)} fusion(f32[256,8,256]{2,1,0:T(8,128)} %reduce_sum.9, f32[256]{0:T(256)S(1)} %copy-done.4, f32[256]{0:T(256)S(1)} %copy-done.5, f32[256]{0:T(256)S(1)} %copy-done.3, f32[256,8,256]{2,0,1:T(8,128)S(1)} %copy.40, f32[256,16,256]{2,0,1:T(8,128)} %copy-done.1, bf16[256,256]{1,0:T(8,128)(2,1)S(1)} %copy-done), kind=kOutput, calls=%fused_computation.12 | convolution fusion | flops 273678336 | bytes 7474176 | tf_op jit(solution)/shard_map/dot_general | solution.py:70
  188.2 1.6 copy.47
  (16 shorter events, 0.2 us)
Async XLA Ops:
  7.2 177.3 %copy-start = (bf16[256,256]{1,0:T(8,128)(2,1)S(1)}, bf16[256,256]{1,0:T(8,128)(2,1)}, u32[]{:S(2)}) copy-start(bf16[256,256]{1,0:T(8,128)(2,1)} %param.18) | copy-start | bytes 393220
  7.2 136.5 %all-gather.3.cloned.1.call-start = ((), (), s32[]{:S(2)}) async-start(), calls=%async_computation.4 | async-start | bytes 9437184 | tf_op jit(solution)/shard_map/all_gather | solution.py:30
  42.8 19.1 %all-to-all-start = ((bf16[8,32,512]{2,1,0:T(8,128)(2,1)}), bf16[8,32,512]{2,1,0:T(8,128)(2,1)S(1)}, u32[]{:S(2)}, u32[]{:S(2)}) async-start(bf16[8,32,512]{2,1,0:T(8,128)(2,1)} %bitcast.46), calls=%async_computation | async-start | bytes 524288 | tf_op jit(solution)/shard_map/all_to_all | solution.py:23
  46.2 134.2 %all-gather.5.cloned.1.call-start = ((), (), s32[]{:S(2)}) async-start(), calls=%async_computation.5 | async-start | bytes 6291456 | tf_op jit(solution)/shard_map/all_gather | solution.py:68
  156.0 5.8 %copy-start.3 = (f32[256]{0:T(256)S(1)}, f32[256]{0:T(256)}, u32[]{:S(2)}) copy-start(f32[256]{0:T(256)} %param.12) | copy-start | bytes 3076
  161.8 1.9 copy-start.1
  163.7 1.0 copy-start.2
  171.7 12.8 %copy-start.4 = (f32[256]{0:T(256)S(1)}, f32[256]{0:T(256)}, u32[]{:S(2)}) copy-start(f32[256]{0:T(256)} %param.19) | copy-start | bytes 3076
  171.7 12.8 %copy-start.5 = (f32[256]{0:T(256)S(1)}, f32[256]{0:T(256)}, u32[]{:S(2)}) copy-start(f32[256]{0:T(256)} %param.17) | copy-start | bytes 3076
Sparse Core Ops, SparseCore 0:
  10.1 133.5 all-gather.2
  168.5 11.8 all-gather.4
